TPU v7x, 256 devices: a whole 4x4x8 slice. The times are simulated.
256 devices in a mesh: tile: 4 (over z_lo, core), freq: 64 (over y, z_hi, x).
Axes of the slice: x: 4, y: 4, z: 8 (z_hi: 4, z_lo: 2; z = z_hi * 2 + z_lo), core: 2. Of those that a mesh axis runs over, the one named last changes fastest.
Arguments:
- sky: bfloat16 [4, 512, 2, 4096], P('tile', 'freq'), may hold values from -6 to 6
- kernel: bfloat16 [4, 64, 2, 4096, 128], P('tile', 'freq'), may hold values from -0.0625 to 0.0625
- data: bfloat16 [64, 2, 128, 512], P('freq'), may hold values from -6 to 6
- block_tiles: int32 [64, 4], P('freq'), may hold values 0 or 1
- length_bin: int32 [64, 128], P('freq'), may hold values from 0 to 31
- wedge_keep: int32 [32, 512], replicated, may hold values 0 or 1
Outputs:
- gradient: float32 [4, 512, 2, 4096], P('tile', 'freq')
All inputs are finite; a program needn't handle non-finite values. No bound on the sum of `block_tiles` on one device may be relied on, other than what follows from the above.
Results may differ from a plain program's by a relative error of at most 0.0027.
Values may be sent and summed in bfloat16 or wider, within the bound.
A program may use at most 128 MiB of HBM per device.

v0:
```python
import math
import jax
import jax.numpy as jnp
from jax import lax
from jax.sharding import Mesh
from jax.sharding import PartitionSpec as P

FREQ = ("freq_0", "freq_1", "freq_2")


def sent_to_all(shard, axis):
    copies = jnp.broadcast_to(shard, (lax.axis_size(axis), *shard.shape))
    return lax.all_to_all(copies, axis, split_axis=0, concat_axis=0, tiled=True)


def of_everyone(shard, axis):
    return sent_to_all(shard, axis).sum(axis=0)


def own_block(tiles, axes, sequence):
    dims = [lax.axis_size(a) for a in axes]
    tiles = tiles.reshape(*dims, *tiles.shape[1:])
    tiles = tiles.transpose(*sequence, *range(len(axes), tiles.ndim))
    tiles = tiles.reshape(-1, *tiles.shape[len(axes) :])
    for k in sequence:
        tiles = lax.psum_scatter(tiles, axes[k], scatter_dimension=0, tiled=True)
    return tiles[0]


def in_blocks(shard, dim, count):
    before, after = (shard.shape[:dim], shard.shape[dim + 1 :])
    return jnp.moveaxis(shard.reshape(*before, count, -1, *after), dim, 0)


def scatter_axes(shard, axes, sequence, dim):
    count = lax.axis_size(axes)
    return own_block(in_blocks(shard, dim, count), axes, sequence)


def delay_tables(length):
    indices = jnp.arange(length, dtype=jnp.int32)
    product = indices[:, None] * indices[None, :] % length
    angle = product.astype(jnp.float32) * (2.0 * math.pi / length)
    return (jnp.cos(angle), jnp.sin(angle))


def real_form(kernel_pair):
    upper_half = jnp.concatenate([kernel_pair[0], kernel_pair[1]], axis=1)
    lower_half = jnp.concatenate([-kernel_pair[1], kernel_pair[0]], axis=1)
    return jnp.concatenate([upper_half, lower_half], axis=0)


def transform(values, table):
    return jnp.einsum("...c,ck->...k", values, table, precision=lax.Precision.HIGHEST)


def keep_table(own_bins, wedge_keep):
    levels = jnp.arange(wedge_keep.shape[0], dtype=jnp.int32)
    one_hot = (own_bins[:, :, None] == levels[None, None, :]).astype(jnp.float32)
    return jnp.einsum(
        "jbl,lk->jbk", one_hot, wedge_keep.astype(jnp.float32), precision=lax.Precision.HIGHEST
    )


def back_project(visibility, data, keep_mask, cosine, sine_table):
    norm_factor = 1.0 / math.sqrt(cosine.shape[0])
    real_vis = visibility[:, 0]
    imag_vis = visibility[:, 1]
    spec_real = (transform(real_vis, cosine) + transform(imag_vis, sine_table)) * norm_factor
    spec_imag = (transform(imag_vis, cosine) - transform(real_vis, sine_table)) * norm_factor
    miss_real = keep_mask * (spec_real - data[:, 0].astype(jnp.float32))
    miss_imag = keep_mask * (spec_imag - data[:, 1].astype(jnp.float32))
    back_real = (transform(miss_real, cosine) - transform(miss_imag, sine_table)) * norm_factor
    back_imag = (transform(miss_imag, cosine) + transform(miss_real, sine_table)) * norm_factor
    return jnp.stack([back_real, back_imag], axis=1).astype(jnp.bfloat16)


def body(sky, kernel, data, block_tiles, length_bin, wedge_keep):
    channels = data.shape[3]
    blocks = kernel.shape[1]
    cell_count = kernel.shape[3]
    base_count = kernel.shape[4]
    local_channels = sky.shape[1]
    tile_pos = lax.axis_index("tile")
    column = jnp.arange(block_tiles.shape[1], dtype=jnp.int32) == tile_pos
    weights = jnp.sum(jnp.where(column[None, :], block_tiles, 0), axis=1).astype(jnp.float32)
    real_forms = jax.vmap(real_form)(kernel[0])
    sky_piece = lax.all_gather(sky, FREQ, axis=1, tiled=True)
    flat_rows = sky_piece[0].reshape(sky_piece.shape[1], 2 * cell_count)
    visibility = jnp.einsum(
        "nc,jcb->jbn", flat_rows, real_forms, preferred_element_type=jnp.float32
    )
    partial_vis = visibility * weights[:, None, None]
    cosine, sine_table = delay_tables(channels)
    visibility = of_everyone(partial_vis, "tile").reshape(blocks, 2, base_count, channels)
    back_field = back_project(
        visibility, data, keep_table(length_bin, wedge_keep), cosine, sine_table
    )
    scaled = (back_field * weights[:, None, None, None].astype(jnp.bfloat16)).reshape(
        blocks, 2 * base_count, channels
    )
    partial_value = jnp.einsum(
        "jpn,jcp->nc", scaled, real_forms, preferred_element_type=jnp.float32
    )
    gradient = scatter_axes(
        partial_value.reshape(local_channels * lax.axis_size(FREQ), 2, cell_count),
        FREQ,
        (0, 2, 1),
        0,
    )
    return gradient[None]


def solution(mesh):
    finer = Mesh(
        mesh.devices.reshape(mesh.shape["tile"], 4, 4, 4), ("tile", "freq_0", "freq_1", "freq_2")
    )
    return jax.shard_map(
        body,
        mesh=finer,
        in_specs=(
            P("tile", FREQ, None, None),
            P("tile", FREQ, None, None, None),
            P(FREQ, None, None, None),
            P(FREQ, None),
            P(FREQ, None),
            P(),
        ),
        out_specs=P("tile", FREQ, None, None),
        check_vma=False,
    )
```

profile of v0, /device:TPU:8, one launch (start us, length us, event | category | flops | bytes accessed | tf_op | source)
XLA Modules:
  0.0 477.6 jit_solution(9158189896188263960)
XLA Ops:
  6.5 0.0 all-gather.2.cloned.1.call-start
  6.5 0.7 all-gather.2.cloned.1.call-update
  7.3 1.3 fusion.40
  9.2 1.4 fusion.73
  10.6 1.7 slice_bitcast_fusion
  12.3 0.0 copy-start
  12.3 0.0 copy-start.1
  12.3 108.5 %all-gather.2.cloned.1.call-done = bf16[1,512,2,4096]{3,2,0,1:T(2,128)(2,1)} async-done(((bf16[1,8,2,4096]{3,2,0,1:T(2,128)(2,1)}), bf16[1,512,2,4096]{3,2,0,1:T(2,128)(2,1)}) %all-gather.2.cloned.1.call-update) | async-done | bytes 8388624 | tf_op jit(solution)/shard_map/all_gather | solution.py:88
  120.7 16.2 %copy.21 = bf16[64,8,2,4096]{3,1,2,0:T(8,128)(2,1)} copy(bf16[64,8,2,4096]{3,2,1,0:T(2,128)(2,1)} %bitcast.61) | data formatting | bytes 16777216
  136.9 0.0 copy-done
  136.9 0.0 copy-done.1
  137.0 0.0 copy-start.2
  137.0 0.0 copy-start.3
  137.0 6.3 %fusion.2 = f32[256,512]{1,0:T(8,128)S(1)} fusion(bf16[512,8192]{1,0:T(8,128)(2,1)} %bitcast.62, f32[]{:T(128)S(6)} %convert_element_type.51, bf16[1,4096,128]{2,1,0:T(8,128)(2,1)S(1)} %get-tuple-element.6, bf16[1,4096,128]{2,1,0:T(8,128)(2,1)S(1)} %fusion.73, bf16[1,4096,128]{2,1,0:T(8,128)(2,1)S(1)} %get-tuple-element.5), kind=kOutput, calls=%fused_computation.7 | convolution fusion | flops 2164391936 | bytes 12058628 | tf_op jit(solution)/shard_map/nc,jcb->jbn/dot_general | solution.py:90
  143.3 1.6 broadcast_in_dim.7
  144.9 10.2 %all-to-all-start = ((f32[4,1,256,512]{3,2,1,0:T(8,128)}), f32[4,1,256,512]{3,2,1,0:T(8,128)S(1)}, u32[]{:S(2)}, u32[]{:S(2)}) async-start(f32[4,1,256,512]{3,2,1,0:T(8,128)} %broadcast_in_dim.7), calls=%async_computation | async-start | bytes 4194304 | tf_op jit(solution)/shard_map/all_to_all | solution.py:13
  155.1 0.0 reduce-scatter.4.cloned.1.call-start
  155.1 0.0 copy-done.2
  155.1 0.0 copy-done.3
  155.1 0.3 fusion.37
  155.4 10.9 %maximum_maximum_fusion = bf16[1,8192,256]{2,1,0:T(8,128)(2,1)} fusion(bf16[1,4096,128]{2,1,0:T(8,128)(2,1)} %copy-done.1, bf16[1,4096,128]{2,1,0:T(8,128)(2,1)S(1)} %fusion.73, bf16[1,4096,128]{2,1,0:T(8,128)(2,1)} %copy-done), kind=kLoop, calls=%fused_computation.1 | loop fusion | flops 16777216 | bytes 7340032 | tf_op jit(solution)/shard_map/vmap()/concatenate | solution.py:50
  166.2 0.0 copy-start.4
  166.2 14.7 %all-to-all-done = f32[4,1,256,512]{3,2,1,0:T(8,128)S(1)} async-done(((f32[4,1,256,512]{3,2,1,0:T(8,128)}), f32[4,1,256,512]{3,2,1,0:T(8,128)S(1)}, u32[]{:S(2)}, u32[]{:S(2)}) %all-to-all-start) | async-done | bytes 2097184 | tf_op jit(solution)/shard_map/all_to_all | solution.py:13
  180.9 0.2 reduce_sum.19
  181.1 4.9 %fusion.27 = f32[128,512]{1,0:T(8,128)S(1)} fusion(f32[1,2,128,512]{3,2,1,0:T(8,128)S(1)} %bitcast.67), kind=kOutput, calls=%fused_computation.35 | convolution fusion | flops 406323200 | bytes 524288 | tf_op jit(solution)/shard_map/...c,ck->...k/dot_general | solution.py:54
  186.0 4.9 %fusion.31 = f32[128,512]{1,0:T(8,128)S(1)} fusion(f32[1,2,128,512]{3,2,1,0:T(8,128)S(1)} %bitcast.68), kind=kOutput, calls=%fused_computation.37 | convolution fusion | flops 406323200 | bytes 524288 | tf_op jit(solution)/shard_map/...c,ck->...k/dot_general | solution.py:54
  190.9 0.0 copy-done.4
  190.9 4.9 %fusion.9 = f32[128,512]{1,0:T(8,128)S(1)} fusion(f32[128,512]{1,0:T(8,128)S(1)} %fusion.37, f32[128,512]{1,0:T(8,128)S(1)} %fusion.27, f32[1,2,128,512]{3,2,1,0:T(8,128)S(1)} %bitcast.69, bf16[1,2,128,512]{3,2,1,0:T(8,128)(2,1)S(1)} %copy-done.4), kind=kOutput, calls=%fused_computation.15 | convolution fusion | flops 406650880 | bytes 1179648 | tf_op jit(solution)/shard_map/...c,ck->...k/dot_general | solution.py:54
  195.7 5.0 %fusion.25 = f32[128,512]{1,0:T(8,128)S(1)} fusion(f32[128,512]{1,0:T(8,128)S(1)} %fusion.9), kind=kOutput, calls=%fused_computation.34 | convolution fusion | flops 406323200 | bytes 524288 | tf_op jit(solution)/shard_map/...c,ck->...k/dot_general | solution.py:54
  200.8 4.9 %fusion.12 = f32[128,512]{1,0:T(8,128)S(1)} fusion(f32[128,512]{1,0:T(8,128)S(1)} %fusion.37, f32[128,512]{1,0:T(8,128)S(1)} %fusion.31, f32[1,2,128,512]{3,2,1,0:T(8,128)S(1)} %bitcast.70, bf16[1,2,128,512]{3,2,1,0:T(8,128)(2,1)S(1)} %copy-done.4), kind=kOutput, calls=%fused_computation.19 | convolution fusion | flops 406650880 | bytes 1179648 | tf_op jit(solution)/shard_map/...c,ck->...k/dot_general | solution.py:54
  205.7 4.9 %fusion.29 = f32[128,512]{1,0:T(8,128)S(1)} fusion(f32[128,512]{1,0:T(8,128)S(1)} %fusion.12), kind=kOutput, calls=%fused_computation.36 | convolution fusion | flops 406323200 | bytes 524288 | tf_op jit(solution)/shard_map/...c,ck->...k/dot_general | solution.py:54
  210.5 4.7 fusion.15
  215.3 4.9 %fusion.16 = bf16[1,1,128,512]{3,2,1,0:T(8,128)(2,1)S(1)} fusion(f32[128,512]{1,0:T(8,128)S(1)} %fusion.29, f32[128,512]{1,0:T(8,128)S(1)} %fusion.9), kind=kOutput, calls=%fused_computation.23 | convolution fusion | flops 406519808 | bytes 655360 | tf_op jit(solution)/shard_map/...c,ck->...k/dot_general | solution.py:54
  220.3 0.1 copy.16
  220.4 4.6 convolution_bitcast_fusion
  225.0 6.2 %copy.17 = f32[4,4,4,8,2,4096]{5,3,4,2,1,0:T(8,128)} copy(f32[4,4,4,8,2,4096]{5,3,4,1,2,0:T(8,128)S(1)} %convolution_bitcast_fusion) | data formatting | bytes 33554432 | tf_op jit(solution)/shard_map/transpose | solution.py:23
  231.2 0.0 reduce-scatter.4.cloned.1.call-update
  231.2 0.0 reduce-scatter.6.cloned.1.call-start
  231.2 148.6 %reduce-scatter.4.cloned.1.call-done = f32[16,8,2,4096]{3,1,2,0:T(8,128)} async-done(((f32[64,8,2,4096]{3,1,2,0:T(8,128)}), f32[16,8,2,4096]{3,1,2,0:T(8,128)}) %reduce-scatter.4.cloned.1.call-update) | async-done | bytes 4194320 | tf_op jit(solution)/shard_map/reduce_scatter | solution.py:26
  379.8 0.0 reduce-scatter.6.cloned.1.call-update
  379.9 0.0 reduce-scatter.8.cloned.1.call-start
  379.9 52.9 %reduce-scatter.6.cloned.1.call-done = f32[4,8,2,4096]{3,1,2,0:T(8,128)} async-done(((f32[16,8,2,4096]{3,1,2,0:T(8,128)}), f32[4,8,2,4096]{3,1,2,0:T(8,128)}) %reduce-scatter.6.cloned.1.call-update) | async-done | bytes 1048592 | tf_op jit(solution)/shard_map/reduce_scatter | solution.py:26
  432.8 0.0 reduce-scatter.8.cloned.1.call-update
  432.8 36.3 %reduce-scatter.8.cloned.1.call-done = f32[1,8,2,4096]{3,1,2,0:T(8,128)} async-done(((f32[4,8,2,4096]{3,1,2,0:T(8,128)}), f32[1,8,2,4096]{3,1,2,0:T(8,128)}) %reduce-scatter.8.cloned.1.call-update) | async-done | bytes 262160 | tf_op jit(solution)/shard_map/reduce_scatter | solution.py:26
  469.0 1.9 copy.18
  (1 shorter events, 0.0 us)
Async XLA Ops:
  6.5 114.2 %all-gather.2.cloned.1.call-start = ((), (), s32[]{:S(2)}) async-start(), calls=%async_computation.4 | async-start | bytes 8519680 | tf_op jit(solution)/shard_map/all_gather | solution.py:88
  12.3 124.7 %copy-start = (bf16[1,4096,128]{2,1,0:T(8,128)(2,1)}, bf16[1,4096,128]{2,1,0:T(8,128)(2,1)S(1)}, u32[]{:S(2)}) copy-start(bf16[1,4096,128]{2,1,0:T(8,128)(2,1)S(1)} %get-tuple-element.5) | copy-start | bytes 3145732
  12.3 124.7 %copy-start.1 = (bf16[1,4096,128]{2,1,0:T(8,128)(2,1)}, bf16[1,4096,128]{2,1,0:T(8,128)(2,1)S(1)}, u32[]{:S(2)}) copy-start(bf16[1,4096,128]{2,1,0:T(8,128)(2,1)S(1)} %get-tuple-element.6) | copy-start | bytes 3145732
  137.0 18.1 %copy-start.2 = (s32[32,512]{1,0:T(8,128)S(1)}, s32[32,512]{1,0:T(8,128)}, u32[]{:S(2)}) copy-start(s32[32,512]{1,0:T(8,128)} %param.11) | copy-start | bytes 196612
  137.0 18.1 %copy-start.3 = (s32[1,128]{1,0:T(1,128)S(1)}, s32[1,128]{1,0:T(1,128)}, u32[]{:S(2)}) copy-start(s32[1,128]{1,0:T(1,128)} %param.10) | copy-start | bytes 1540
  144.9 36.0 %all-to-all-start = ((f32[4,1,256,512]{3,2,1,0:T(8,128)}), f32[4,1,256,512]{3,2,1,0:T(8,128)S(1)}, u32[]{:S(2)}, u32[]{:S(2)}) async-start(f32[4,1,256,512]{3,2,1,0:T(8,128)} %broadcast_in_dim.7), calls=%async_computation | async-start | bytes 4194304 | tf_op jit(solution)/shard_map/all_to_all | solution.py:13
  155.1 224.8 %reduce-scatter.4.cloned.1.call-start = ((), (), s32[]{:S(2)}) async-start(), calls=%async_computation.5 | async-start | bytes 20971520 | tf_op jit(solution)/shard_map/reduce_scatter | solution.py:26
  166.2 24.6 %copy-start.4 = (bf16[1,2,128,512]{3,2,1,0:T(8,128)(2,1)S(1)}, bf16[1,2,128,512]{3,2,1,0:T(8,128)(2,1)}, u32[]{:S(2)}) copy-start(bf16[1,2,128,512]{3,2,1,0:T(8,128)(2,1)} %param.8) | copy-start | bytes 786436
  231.2 201.6 %reduce-scatter.6.cloned.1.call-start = ((), (), s32[]{:S(2)}) async-start(), calls=%async_computation.6 | async-start | bytes 5242880 | tf_op jit(solution)/shard_map/reduce_scatter | solution.py:26
  379.9 89.2 %reduce-scatter.8.cloned.1.call-start = ((), (), s32[]{:S(2)}) async-start(), calls=%async_computation.7 | async-start | bytes 1310720 | tf_op jit(solution)/shard_map/reduce_scatter | solution.py:26
Sparse Core Ops, SparseCore 0:
  10.6 110.0 all-gather.1
  231.3 148.4 reduce-scatter.3
  382.4 50.3 reduce-scatter.5
  435.2 33.8 reduce-scatter.7
where the time goes:
time: 487 us; the launch traced here: 478 us
  waiting for transfers between devices  362 us (74%)
  matrix products  50.2 us (10%)
  local copies, waits for them, and re-layouts  27.7 us (6%)
  between operations  14.2 us (3%)
  other arithmetic  13.8 us (3%)
  starting transfers between devices  10.3 us (2%)
    reduce_scatter x3, waiting for transfers between devices, own_block(): tiles = lax.psum_scatter(tiles, axes[k], scatter_dimension=0, tiled=True)  238 us
    all_gather x1, waiting for transfers between devices, body(): sky_piece = lax.all_gather(sky, FREQ, axis=1, tiled=True)  108 us
    dot_general x8, matrix products, transform(): jnp.einsum('...c,ck->...k', values, table, precision=lax.Precision.HIGHEST)  39 us
    unnamed x11, local copies, waits for them, and re-layouts  16.2 us
    all_to_all x1, waiting for transfers between devices, sent_to_all(): return lax.all_to_all(copies, axis, split_axis=0, concat_axis=0, tiled=True)  14.7 us
    concatenate x1, other arithmetic, real_form(): return jnp.concatenate([upper_half, lower_half], axis=0)  10.9 us
    all_to_all x1, starting transfers between devices, sent_to_all(): return lax.all_to_all(copies, axis, split_axis=0, concat_axis=0, tiled=True)  10.2 us
  transfers between devices with their start and end apart: 5, of which 5 were waited for; matrix products, arithmetic and copies ran while one was open for 3% of the time, Pallas kernels for 0%

commit v1 on v0

--- a/solution.py
+++ b/solution.py
@@ -85,7 +85,9 @@
     column = jnp.arange(block_tiles.shape[1], dtype=jnp.int32) == tile_pos
     weights = jnp.sum(jnp.where(column[None, :], block_tiles, 0), axis=1).astype(jnp.float32)
     real_forms = jax.vmap(real_form)(kernel[0])
-    sky_piece = lax.all_gather(sky, FREQ, axis=1, tiled=True)
+    sky_piece = jnp.concatenate(
+        lax.all_to_all(jnp.stack([sky] * lax.axis_size(FREQ)), FREQ, 0, 0), axis=1
+    )
     flat_rows = sky_piece[0].reshape(sky_piece.shape[1], 2 * cell_count)
     visibility = jnp.einsum(
         "nc,jcb->jbn", flat_rows, real_forms, preferred_element_type=jnp.float32

time: 487 us -> 574 us (1.18)
  waiting for transfers between devices: 362 us -> 435 us
  starting transfers between devices: 10.3 us -> 19 us
  local copies, waits for them, and re-layouts: 27.7 us -> 34.1 us
    all_to_all x0 -> x1, waiting for transfers between devices: none -> 182 us  [body(): lax.all_to_all(jnp.stack([sky] * lax.axis_size(FREQ)), FREQ, 0, 0)]
    all_gather x1 -> x0, waiting for transfers between devices: 108 us -> none  [body(): sky_piece = lax.all_gather(sky, FREQ, axis=1, tiled=True)]
    all_to_all x0 -> x1, starting transfers between devices: none -> 14.9 us  [body(): lax.all_to_all(jnp.stack([sky] * lax.axis_size(FREQ)), FREQ, 0, 0)]
    another operation x0 -> x1, local copies, waits for them, and re-layouts: none -> 6.42 us  [body(): jnp.stack([sky] * lax.axis_size(FREQ))]
    all_to_all x1, starting transfers between devices: 10.2 us -> 4.01 us  [sent_to_all(): return lax.all_to_all(copies, axis, split_axis=0, concat_axis=0, tiled=True)]
    unnamed x11 -> x15, local copies, waits for them, and re-layouts: 16.2 us -> 16.4 us
  transfers between devices with their start and end apart: 5 -> 5, of which waited for: 5 -> 5; matrix products, arithmetic and copies ran while one was open for 3% -> 2% of each run, Pallas kernels for 0% -> 0%
where the time goes in v1:
time: 574 us; the launch traced here: 564 us
  waiting for transfers between devices  435 us (76%)
  matrix products  50 us (9%)
  local copies, waits for them, and re-layouts  34.1 us (6%)
  starting transfers between devices  19 us (3%)
  between operations  14.4 us (3%)
  other arithmetic  11.9 us (2%)
    reduce_scatter x3, waiting for transfers between devices, own_block(): tiles = lax.psum_scatter(tiles, axes[k], scatter_dimension=0, tiled=True)  239 us
    all_to_all x1, waiting for transfers between devices, body(): lax.all_to_all(jnp.stack([sky] * lax.axis_size(FREQ)), FREQ, 0, 0)  182 us
    dot_general x8, matrix products, transform(): jnp.einsum('...c,ck->...k', values, table, precision=lax.Precision.HIGHEST)  39.1 us
    unnamed x15, local copies, waits for them, and re-layouts  16.4 us
    all_to_all x1, starting transfers between devices, body(): lax.all_to_all(jnp.stack([sky] * lax.axis_size(FREQ)), FREQ, 0, 0)  14.9 us
    all_to_all x1, waiting for transfers between devices, sent_to_all(): return lax.all_to_all(copies, axis, split_axis=0, concat_axis=0, tiled=True)  14.5 us
  transfers between devices with their start and end apart: 5, of which 5 were waited for; matrix products, arithmetic and copies ran while one was open for 2% of the time, Pallas kernels for 0%

profile of v1, /device:TPU:8, one launch (start us, length us, event | category | flops | bytes accessed | tf_op | source)
XLA Modules:
  0.0 564.1 jit_solution(16455675858829789407)
XLA Ops:
  6.5 6.4 %stack.8 = bf16[64,1,8,2,4096]{4,3,2,1,0:T(2,128)(2,1)} broadcast(bf16[8,2,4096]{2,1,0:T(2,128)(2,1)} %bitcast.70), dimensions={2,3,4} | broadcast | bytes 8519680 | tf_op jit(solution)/shard_map/stack | solution.py:89
  13.0 0.0 copy-start.6
  13.0 0.0 copy-start
  13.0 14.9 %all-to-all-start = ((bf16[64,1,8,2,4096]{4,3,2,1,0:T(2,128)(2,1)}), bf16[64,1,8,2,4096]{4,3,2,1,0:T(2,128)(2,1)}, u32[]{:S(2)}, u32[]{:S(2)}) async-start(bf16[64,1,8,2,4096]{4,3,2,1,0:T(2,128)(2,1)} %stack.8), calls=%async_computation | async-start | bytes 16777216 | tf_op jit(solution)/shard_map/all_to_all | solution.py:89
  27.9 0.0 copy-done.6
  27.9 0.6 fusion.40
  29.2 0.0 copy-done
  29.2 0.1 fusion.73
  29.3 1.5 slice_bitcast_fusion
  30.8 181.5 %all-to-all-done = bf16[64,1,8,2,4096]{4,3,2,1,0:T(2,128)(2,1)} async-done(((bf16[64,1,8,2,4096]{4,3,2,1,0:T(2,128)(2,1)}), bf16[64,1,8,2,4096]{4,3,2,1,0:T(2,128)(2,1)}, u32[]{:S(2)}, u32[]{:S(2)}) %all-to-all-start) | async-done | bytes 8388640 | tf_op jit(solution)/shard_map/all_to_all | solution.py:89
  212.4 0.0 copy-start.1
  212.4 16.4 %copy.16 = bf16[64,8,2,4096]{3,1,2,0:T(8,128)(2,1)} copy(bf16[64,8,2,4096]{3,2,1,0:T(2,128)(2,1)} %bitcast.31) | data formatting | bytes 16777216
  228.7 0.0 copy-done.1
  228.7 0.0 copy-done.2
  228.8 0.0 copy-start.3
  228.8 0.0 copy-start.4
  228.8 6.1 %fusion.2 = f32[256,512]{1,0:T(8,128)S(1)} fusion(bf16[512,8192]{1,0:T(8,128)(2,1)} %bitcast.60, f32[]{:T(128)S(6)} %convert_element_type.51, bf16[1,4096,128]{2,1,0:T(8,128)(2,1)S(1)} %copy-done.2, bf16[1,4096,128]{2,1,0:T(8,128)(2,1)S(1)} %fusion.73, bf16[1,4096,128]{2,1,0:T(8,128)(2,1)S(1)} %copy-done.1), kind=kOutput, calls=%fused_computation.7 | convolution fusion | flops 2164391936 | bytes 12058628 | tf_op jit(solution)/shard_map/nc,jcb->jbn/dot_general | solution.py:92
  234.8 1.6 broadcast_in_dim.7
  236.4 4.0 all-to-all-start.1
  240.4 0.0 reduce-scatter.4.cloned.1.call-start
  240.4 0.0 copy-done.3
  240.4 0.0 copy-done.4
  240.5 0.3 fusion.37
  240.8 10.9 %maximum_maximum_fusion = bf16[1,8192,256]{2,1,0:T(8,128)(2,1)} fusion(bf16[1,4096,128]{2,1,0:T(8,128)(2,1)} %get-tuple-element.6, bf16[1,4096,128]{2,1,0:T(8,128)(2,1)S(1)} %fusion.73, bf16[1,4096,128]{2,1,0:T(8,128)(2,1)} %get-tuple-element.5), kind=kLoop, calls=%fused_computation.1 | loop fusion | flops 16777216 | bytes 7340032 | tf_op jit(solution)/shard_map/vmap()/concatenate | solution.py:50
  251.6 0.0 copy-start.5
  251.6 14.5 %all-to-all-done.1 = f32[4,1,256,512]{3,2,1,0:T(8,128)S(1)} async-done(((f32[4,1,256,512]{3,2,1,0:T(8,128)}), f32[4,1,256,512]{3,2,1,0:T(8,128)S(1)}, u32[]{:S(2)}, u32[]{:S(2)}) %all-to-all-start.1) | async-done | bytes 2097184 | tf_op jit(solution)/shard_map/all_to_all | solution.py:13
  266.1 0.2 reduce_sum.19
  266.4 4.9 fusion.27
  271.2 4.9 fusion.31
  276.1 0.0 copy-done.5
  276.1 4.9 fusion.9
  281.0 5.1 fusion.25
  286.0 4.9 fusion.12
  290.9 4.9 fusion.29
  295.8 4.7 fusion.15
  300.5 5.0 fusion.16
  305.6 0.1 copy.11
  305.7 4.6 convolution_bitcast_fusion
  310.3 6.2 %copy.12 = f32[4,4,4,8,2,4096]{5,3,4,2,1,0:T(8,128)} copy(f32[4,4,4,8,2,4096]{5,3,4,1,2,0:T(8,128)S(1)} %convolution_bitcast_fusion) | data formatting | bytes 33554432 | tf_op jit(solution)/shard_map/transpose | solution.py:23
  316.5 0.0 reduce-scatter.4.cloned.1.call-update
  316.5 0.0 reduce-scatter.6.cloned.1.call-start
  316.6 149.7 %reduce-scatter.4.cloned.1.call-done = f32[16,8,2,4096]{3,1,2,0:T(8,128)} async-done(((f32[64,8,2,4096]{3,1,2,0:T(8,128)}), f32[16,8,2,4096]{3,1,2,0:T(8,128)}) %reduce-scatter.4.cloned.1.call-update) | async-done | bytes 4194320 | tf_op jit(solution)/shard_map/reduce_scatter | solution.py:26
  466.2 0.0 reduce-scatter.6.cloned.1.call-update
  466.3 0.0 reduce-scatter.8.cloned.1.call-start
  466.3 52.9 %reduce-scatter.6.cloned.1.call-done = f32[4,8,2,4096]{3,1,2,0:T(8,128)} async-done(((f32[16,8,2,4096]{3,1,2,0:T(8,128)}), f32[4,8,2,4096]{3,1,2,0:T(8,128)}) %reduce-scatter.6.cloned.1.call-update) | async-done | bytes 1048592 | tf_op jit(solution)/shard_map/reduce_scatter | solution.py:26
  519.2 0.0 reduce-scatter.8.cloned.1.call-update
  519.2 36.1 %reduce-scatter.8.cloned.1.call-done = f32[1,8,2,4096]{3,1,2,0:T(8,128)} async-done(((f32[4,8,2,4096]{3,1,2,0:T(8,128)}), f32[1,8,2,4096]{3,1,2,0:T(8,128)}) %reduce-scatter.8.cloned.1.call-update) | async-done | bytes 262160 | tf_op jit(solution)/shard_map/reduce_scatter | solution.py:26
  555.3 1.9 copy.13
  (2 shorter events, 0.0 us)
Async XLA Ops:
  13.0 14.9 %copy-start.6 = (s32[1,4]{1,0:T(1,128)S(1)}, s32[1,4]{1,0:T(1,128)}, u32[]{:S(2)}) copy-start(s32[1,4]{1,0:T(1,128)} %param.9) | copy-start | bytes 52
  13.0 16.2 %copy-start = (bf16[1,1,2,4096,128]{4,3,2,1,0:T(8,128)(2,1)S(1)}, bf16[1,1,2,4096,128]{4,3,2,1,0:T(8,128)(2,1)}, u32[]{:S(2)}) copy-start(bf16[1,1,2,4096,128]{4,3,2,1,0:T(8,128)(2,1)} %param.7) | copy-start | bytes 6291460
  13.0 199.4 %all-to-all-start = ((bf16[64,1,8,2,4096]{4,3,2,1,0:T(2,128)(2,1)}), bf16[64,1,8,2,4096]{4,3,2,1,0:T(2,128)(2,1)}, u32[]{:S(2)}, u32[]{:S(2)}) async-start(bf16[64,1,8,2,4096]{4,3,2,1,0:T(2,128)(2,1)} %stack.8), calls=%async_computation | async-start | bytes 16777216 | tf_op jit(solution)/shard_map/all_to_all | solution.py:89
  212.4 16.4 %copy-start.1 = (bf16[1,4096,128]{2,1,0:T(8,128)(2,1)S(1)}, bf16[1,4096,128]{2,1,0:T(8,128)(2,1)}, u32[]{:S(2)}) copy-start(bf16[1,4096,128]{2,1,0:T(8,128)(2,1)} %get-tuple-element.5) | copy-start | bytes 3145732
  212.4 16.4 %copy-start.2 = (bf16[1,4096,128]{2,1,0:T(8,128)(2,1)S(1)}, bf16[1,4096,128]{2,1,0:T(8,128)(2,1)}, u32[]{:S(2)}) copy-start(bf16[1,4096,128]{2,1,0:T(8,128)(2,1)} %get-tuple-element.6) | copy-start | bytes 3145732
  228.8 11.7 %copy-start.3 = (s32[32,512]{1,0:T(8,128)S(1)}, s32[32,512]{1,0:T(8,128)}, u32[]{:S(2)}) copy-start(s32[32,512]{1,0:T(8,128)} %param.11) | copy-start | bytes 196612
  228.8 11.7 %copy-start.4 = (s32[1,128]{1,0:T(1,128)S(1)}, s32[1,128]{1,0:T(1,128)}, u32[]{:S(2)}) copy-start(s32[1,128]{1,0:T(1,128)} %param.10) | copy-start | bytes 1540
  236.4 29.7 %all-to-all-start.1 = ((f32[4,1,256,512]{3,2,1,0:T(8,128)}), f32[4,1,256,512]{3,2,1,0:T(8,128)S(1)}, u32[]{:S(2)}, u32[]{:S(2)}) async-start(f32[4,1,256,512]{3,2,1,0:T(8,128)} %broadcast_in_dim.7), calls=%async_computation.1 | async-start | bytes 4194304 | tf_op jit(solution)/shard_map/all_to_all | solution.py:13
  240.4 225.8 %reduce-scatter.4.cloned.1.call-start = ((), (), s32[]{:S(2)}) async-start(), calls=%async_computation.5 | async-start | bytes 20971520 | tf_op jit(solution)/shard_map/reduce_scatter | solution.py:26
  251.6 24.5 %copy-start.5 = (bf16[1,2,128,512]{3,2,1,0:T(8,128)(2,1)S(1)}, bf16[1,2,128,512]{3,2,1,0:T(8,128)(2,1)}, u32[]{:S(2)}) copy-start(bf16[1,2,128,512]{3,2,1,0:T(8,128)(2,1)} %param.8) | copy-start | bytes 786436
  316.5 202.7 %reduce-scatter.6.cloned.1.call-start = ((), (), s32[]{:S(2)}) async-start(), calls=%async_computation.6 | async-start | bytes 5242880 | tf_op jit(solution)/shard_map/reduce_scatter | solution.py:26
  466.3 89.0 %reduce-scatter.8.cloned.1.call-start = ((), (), s32[]{:S(2)}) async-start(), calls=%async_computation.7 | async-start | bytes 1310720 | tf_op jit(solution)/shard_map/reduce_scatter | solution.py:26
Sparse Core Ops, SparseCore 0:
  316.6 149.5 reduce-scatter.3
  468.8 50.3 reduce-scatter.5
  521.7 33.5 reduce-scatter.7
